TPU v7x, 32 devices: a whole 2x2x4 slice. The times are simulated.
32 devices in a mesh: seq: 8 (over z, y), head: 4 (over x, core).
Axes of the slice: x: 2, y: 2, z: 4, core: 2. Of those that a mesh axis runs over, the one named last changes fastest.
Arguments:
- tokens: bfloat16 [2048, 2560], P('seq'), may hold values from -6 to 6
- x_weight: bfloat16 [2560, 5120], P(None, 'head'), may hold values from -0.125 to 0.125
- b_input: bfloat16 [2048, 128], P('seq'), may hold values from -6 to 6
- c_input: bfloat16 [2048, 128], P('seq'), may hold values from -0.52734375 to 0.52734375
- log_decay: float32 [2048, 80], P('seq', 'head'), may hold values from -1 to 0
- step_size: float32 [2048, 80], P('seq', 'head'), may hold values from 0 to 1
- cotangent: bfloat16 [2048, 5120], P('seq', 'head'), may hold values from -6 to 6
Outputs:
- ssd_out: bfloat16 [2048, 5120], P('seq', 'head')
- tokens_grad: bfloat16 [2048, 2560], P('seq', 'head')
- weight_grad: float32 [2560, 5120], P('seq', 'head')
- decay_grad: float32 [2048, 80], P('seq', 'head')
All inputs are finite; a program needn't handle non-finite values.
Results may differ from a plain program's by a relative error of at most 0.0061.
Values sent between devices are 32-bit elements; how exact they have to be, the bound alone decides.
A program may use at most 192 MiB of HBM per device.

v0:
```python
import jax
import jax.numpy as jnp
from jax import lax
from jax.sharding import PartitionSpec as P

SPAN = 256


highest = lax.Precision.HIGHEST


def carried_in(part, axis, combine, identity, reverse):
    count = lax.axis_size(axis)
    place = lax.axis_index(axis)
    ahead = count - 1 - place if reverse else place
    gathered = jax.tree.map(lambda a: lax.all_gather(a, axis), part)
    state = jax.tree.map(lambda a, e: jnp.zeros_like(a) + jnp.asarray(e, a.dtype), part, identity)

    def one(step, state):
        source = count - 1 - step if reverse else step
        return combine(
            state, jax.tree.map(lambda a: lax.dynamic_index_in_dim(a, source, 0, False), gathered)
        )

    return lax.fori_loop(0, ahead, one, state)


def span_tables(length):
    row_ids = lax.broadcasted_iota(jnp.int32, (length, length), 0)
    col_ids = lax.broadcasted_iota(jnp.int32, (length, length), 1)
    return (row_ids >= col_ids, row_ids > col_ids)


def combine_pairs(first_part, second_part):
    return (
        first_part[0] * second_part[0],
        second_part[0][:, None, None] * first_part[1] + second_part[1],
    )


def weight_rows(inputs, gradients):
    return lax.dot_general(
        inputs, gradients, (((0,), (0,)), ((), ())), preferred_element_type=jnp.float32
    )


def per_device(tokens, x_weight, b_input, c_input, log_decay, step_size, cotangent):
    tok_rows = tokens.shape[0]
    head_count = log_decay.shape[1]
    head_width = cotangent.shape[1] // head_count
    blocks = tok_rows // SPAN
    pre_act = jnp.dot(tokens, x_weight, preferred_element_type=jnp.float32)
    activated = jax.nn.silu(pre_act)
    x_scaled = (activated.reshape(tok_rows, head_count, head_width) * step_size[:, :, None]).astype(
        jnp.bfloat16
    )
    lower_mask, strict_mask = span_tables(SPAN)
    lower_ones = lower_mask.astype(jnp.float32)
    strict_ones = strict_mask.astype(jnp.float32)
    cum_log = jnp.einsum(
        "qr,krh->kqh", lower_ones, log_decay.reshape(blocks, SPAN, head_count), precision=highest
    )
    x_blocks = x_scaled.reshape(blocks, SPAN, head_count, head_width)
    grad_blocks = cotangent.reshape(blocks, SPAN, head_count, head_width)
    b_blocks = b_input.reshape(blocks, SPAN, b_input.shape[1])
    c_blocks = c_input.reshape(blocks, SPAN, c_input.shape[1])
    span_ends = cum_log[:, -1, :]
    factors = jnp.exp(span_ends)
    b_weighted = (
        jnp.exp(span_ends[:, None, :] - cum_log)[..., None]
        * b_blocks.astype(jnp.float32)[:, :, None, :]
    ).astype(jnp.bfloat16)
    c_weighted = (jnp.exp(cum_log)[..., None] * c_blocks.astype(jnp.float32)[:, :, None, :]).astype(
        jnp.bfloat16
    )
    local_states = jnp.einsum(
        "kqhn,kqhp->khnp", b_weighted, x_blocks, preferred_element_type=jnp.float32
    )
    local_grads = jnp.einsum(
        "kqhn,kqhp->khnp", c_weighted, grad_blocks, preferred_element_type=jnp.float32
    )
    unit_decay = jnp.ones((head_count,), jnp.float32)
    zero_state = jnp.zeros(local_states.shape[1:], jnp.float32)
    total_decay = unit_decay
    total_state = zero_state
    block_index = 0
    total_state = factors[block_index][:, None, None] * total_state + local_states[block_index]
    total_decay = total_decay * factors[block_index]
    entering = carried_in(
        (total_decay, total_state), "seq", combine_pairs, (unit_decay, zero_state), False
    )[1]
    back_decay = unit_decay
    back_state = zero_state
    for block_index in reversed(range(blocks)):
        back_state = local_grads[block_index] + factors[block_index][:, None, None] * back_state
        back_decay = back_decay * factors[block_index]
    leaving = carried_in(
        (back_decay, back_state), "seq", combine_pairs, (unit_decay, zero_state), True
    )[1]
    running = entering
    block_index = 0
    priors = [running]
    prior_states = jnp.stack(priors)
    adjoints = [zero_state] * blocks
    running = leaving
    for block_index in reversed(range(blocks)):
        adjoints[block_index] = running
        running = local_grads[block_index] + factors[block_index][:, None, None] * running
    later_adjoints = jnp.stack(adjoints)
    scores = jnp.einsum("kqn,krn->kqr", c_blocks, b_blocks, preferred_element_type=jnp.float32)
    cum_heads = jnp.transpose(cum_log, (0, 2, 1))
    log_gap = cum_heads[..., :, None] - cum_heads[..., None, :]
    mixing = scores[:, None] * jnp.exp(jnp.where(lower_mask, log_gap, -jnp.inf))
    rounded = mixing.astype(jnp.bfloat16)
    inner_part = jnp.einsum(
        "khqr,krhp->kqhp", rounded, x_blocks, preferred_element_type=jnp.float32
    )
    carried = jnp.einsum(
        "kqhn,khnp->kqhp", c_weighted.astype(jnp.float32), prior_states, precision=highest
    )
    ssd_out = (inner_part + carried).astype(jnp.bfloat16).reshape(tok_rows, head_count * head_width)
    back_inner = jnp.einsum(
        "khqr,kqhp->krhp", rounded, grad_blocks, preferred_element_type=jnp.float32
    )
    back_carried = jnp.einsum(
        "krhn,khnp->krhp", b_weighted.astype(jnp.float32), later_adjoints, precision=highest
    )
    grad_x = back_inner + back_carried
    products = jnp.einsum(
        "kqhp,krhp->khqr", grad_blocks, x_blocks, preferred_element_type=jnp.float32
    )
    pair_terms = jnp.where(strict_mask, mixing * products, 0.0)
    shifts = jnp.transpose(jnp.sum(pair_terms, axis=3) - jnp.sum(pair_terms, axis=2), (0, 2, 1))
    arrival = jnp.sum(grad_blocks.astype(jnp.float32) * carried, axis=3)
    departure = jnp.sum(x_blocks.astype(jnp.float32) * back_carried, axis=3)
    through = factors * jnp.sum(prior_states * later_adjoints, axis=(2, 3))
    decay_grad = jnp.einsum("tj,kth->kjh", lower_ones, shifts + arrival, precision=highest)
    decay_grad = (
        decay_grad
        + jnp.einsum("jr,krh->kjh", strict_ones, departure, precision=highest)
        + through[:, None, :]
    )
    decay_grad = decay_grad.reshape(tok_rows, head_count)
    sigmoid_pre = jax.nn.sigmoid(pre_act)
    scaled_grad = (
        grad_x.reshape(tok_rows, head_count, head_width) * step_size[:, :, None]
    ).reshape(tok_rows, head_count * head_width)
    pre_grad = (scaled_grad * sigmoid_pre * (1.0 + pre_act * (1.0 - sigmoid_pre))).astype(
        jnp.bfloat16
    )
    weight_grad = lax.psum_scatter(
        weight_rows(tokens, pre_grad), "seq", scatter_dimension=0, tiled=True
    )
    partial_grad = lax.dot_general(
        pre_grad, x_weight, (((1,), (1,)), ((), ())), preferred_element_type=jnp.float32
    )
    tokens_grad = lax.psum_scatter(partial_grad, "head", scatter_dimension=1, tiled=True).astype(
        jnp.bfloat16
    )
    return (ssd_out, tokens_grad, weight_grad, decay_grad)


def solution(mesh):
    return jax.shard_map(
        per_device,
        mesh=mesh,
        in_specs=(
            P("seq", None),
            P(None, "head"),
            P("seq", None),
            P("seq", None),
            P("seq", "head"),
            P("seq", "head"),
            P("seq", "head"),
        ),
        out_specs=(P("seq", "head"), P("seq", "head"), P("seq", "head"), P("seq", "head")),
        check_vma=False,
    )
```

profile of v0, /device:TPU:0, one launch (start us, length us, event | category | flops | bytes accessed | tf_op | source)
XLA Modules:
  0.0 499.4 jit_solution(14164791766661126989)
XLA Ops:
  7.2 1.0 fusion.54
  9.1 0.9 convert_element_type.87
  10.0 1.3 copy.51
  11.4 1.9 fusion.48
  13.6 1.5 copy.56
  15.1 22.4 %all-gather = f32[8,1,20]{2,1,0:T(1,128)S(1)} all-gather(f32[1,1,20]{2,1,0:T(1,128)S(1)} %copy.48), channel_id=2, replica_groups=mesh['seq'=8,'head'=4] {'seq'}, dimensions={0}, use_global_device_ids=true | all-gather | bytes 720 | tf_op jit(solution)/shard_map/all_gather | solution.py:16
  38.2 0.9 fusion.61
  39.1 63.4 %all-gather.8.cloned.1.call-done = f32[160,128,64]{1,2,0:T(8,128)} async-done(((f32[20,128,64]{1,2,0:T(8,128)}), f32[160,128,64]{1,2,0:T(8,128)}) %all-gather.8.cloned.1.call-update) | async-done | bytes 5242896 | tf_op jit(solution)/shard_map/all_gather | solution.py:16
  102.5 1.2 broadcast_in_dim.35.clone
  103.7 28.9 %while.27 = (s32[]{:T(128)}, f32[20,128,64]{2,1,0:T(8,128)}, s32[]{:T(128)}, f32[8,20]{1,0:T(8,128)S(1)}, f32[8,20,128,64]{2,3,1,0:T(8,128)}, /*index=5*/s32[]{:T(128)}, s32[]{:T(128)}, s32[]{:T(128)}, s32[]{:T(128)}) while((s32[]{:T(128)}, f32[20,128,64]{2,1,0:T(8,128)}, s32[]{:T(128)}, f32[8,20]{1,0:T(8,128)S(1)}, ...), condition=%wide.region_3.4_spmd, body=%wide.region_2.3_spmd.sunk | while | flops 327686 | bytes 4587915 | solution.py:25
  103.7 1.1 constant_dynamic-slice_fusion.5
  105.2 2.6 bitcast_add_fusion.6
  107.8 1.1 constant_dynamic-slice_fusion.5
  109.3 2.6 bitcast_add_fusion.6
  111.9 1.1 constant_dynamic-slice_fusion.5
  113.5 2.6 bitcast_add_fusion.6
  116.0 1.1 constant_dynamic-slice_fusion.5
  117.6 2.6 bitcast_add_fusion.6
  120.2 1.1 constant_dynamic-slice_fusion.5
  121.7 2.6 bitcast_add_fusion.6
  124.3 1.1 constant_dynamic-slice_fusion.5
  125.8 2.6 bitcast_add_fusion.6
  128.4 1.1 constant_dynamic-slice_fusion.5
  130.0 2.6 bitcast_add_fusion.6
  132.5 3.6 fusion.29
  136.2 2.6 fusion.30
  138.8 2.9 copy.55
  141.6 6.4 %multiply_convert_fusion.11 = (bf16[256,1280]{1,0:T(8,128)(2,1)S(1)}, f32[256,1280]{1,0:T(8,128)}) fusion(f32[256,1280]{1,0:T(8,128)} %copy.55, f32[256,1280]{1,0:T(8,128)S(1)} %copy-done.5, bf16[256,2560]{1,0:T(8,128)(2,1)S(1)} %copy-done, bf16[2560,1280]{1,0:T(8,128)(2,1)} %param.12), kind=kOutput, calls=%fused_computation.42 | convolution fusion | flops 1681326080 | bytes 12451840 | tf_op jit(solution)/shard_map/dot_general | solution.py:52
  148.0 6.2 %fusion.62 = f32[256,2560]{1,0:T(8,128)} fusion(bf16[256,1280]{1,0:T(8,128)(2,1)S(1)} %get-tuple-element.198, bf16[2560,1280]{1,0:T(8,128)(2,1)} %param.12), kind=kOutput, calls=%fused_computation.77 | convolution fusion | flops 1677721600 | bytes 9830400 | tf_op jit(solution)/shard_map/dot_general | solution.py:154
  154.3 1.7 copy.45
  156.1 0.9 multiply_convert_fusion.12
  157.0 0.9 copy-done.9
  157.8 1.9 fusion.49
  160.0 6.7 %convolution_bitcast_fusion = f32[2560,1280]{0,1:T(8,128)} fusion(bf16[256,1280]{1,0:T(8,128)(2,1)S(1)} %get-tuple-element.198, bf16[256,2560]{1,0:T(8,128)(2,1)S(1)} %copy-done), kind=kOutput, calls=%fused_computation.6 | convolution fusion | flops 1677721600 | bytes 15073280 | tf_op jit(solution)/shard_map/dot_general | solution.py:42
  166.7 14.1 %copy.67 = f32[2560,1280]{1,0:T(8,128)} copy(f32[2560,1280]{0,1:T(8,128)} %convolution_bitcast_fusion) | data formatting | bytes 26214400
  180.8 1.0 copy-done.4
  181.8 1.3 copy.57
  183.2 0.9 multiply_reduce_fusion.1
  184.5 3.0 fusion.2
  187.5 1.8 convert_element_type.91
  189.4 86.3 %all-gather.6.cloned.1.call-done = f32[160,128,64]{1,2,0:T(8,128)} async-done(((f32[20,128,64]{1,2,0:T(8,128)}), f32[160,128,64]{1,2,0:T(8,128)}) %all-gather.6.cloned.1.call-update) | async-done | bytes 5242896 | tf_op jit(solution)/shard_map/all_gather | solution.py:16
  275.8 0.7 copy-done.20
  276.5 3.6 multiply_reduce_fusion.2
  280.2 1.6 fusion.36
  281.7 1.1 copy.60
  282.8 1.6 multiply_reduce_fusion
  285.0 0.8 fusion.52
  285.8 207.0 %reduce-scatter.7.cloned.1.call-done = f32[320,1280]{1,0:T(8,128)} async-done(((f32[2560,1280]{1,0:T(8,128)}), f32[320,1280]{1,0:T(8,128)}) %reduce-scatter.7.cloned.1.call-update) | async-done | bytes 1638416
  (94 shorter events, 6.3 us)
Async XLA Ops:
  7.2 134.5 %copy-start = (bf16[256,2560]{1,0:T(8,128)(2,1)S(1)}, bf16[256,2560]{1,0:T(8,128)(2,1)}, u32[]{:S(2)}) copy-start(bf16[256,2560]{1,0:T(8,128)(2,1)} %param.11) | copy-start | bytes 3932164
  7.2 95.3 %all-gather.8.cloned.1.call-start = ((), (), s32[]{:S(2)}) async-start(), calls=%async_computation.4 | async-start | bytes 5898240 | tf_op jit(solution)/shard_map/all_gather | solution.py:16
  8.2 0.9 copy-start.22
  9.1 4.2 copy-start.19
  11.3 2.1 copy-start.6
  11.4 2.1 copy-start.16
  11.4 2.1 copy-start.17
  13.3 174.2 %reduce-scatter.5.cloned.1.call-start = ((), (), s32[]{:S(2)}) async-start(), calls=%async_computation.2 | async-start | bytes 3276800 | tf_op jit(solution)/shard_map/reduce_scatter | solution.py:157
  13.6 24.6 %copy-start.15 = (bf16[256,128]{1,0:T(8,128)(2,1)S(1)}, bf16[256,128]{1,0:T(8,128)(2,1)}, u32[]{:S(2)}) copy-start(bf16[256,128]{1,0:T(8,128)(2,1)} %param.14) | copy-start | bytes 196612
  132.5 3.6 copy-start.7
  132.5 3.6 copy-start.12
  132.5 3.6 copy-start.23
  132.5 3.6 copy-start.25
  136.1 2.6 copy-start.2
  138.8 2.9 copy-start.5
  154.3 121.4 %all-gather.6.cloned.1.call-start = ((), (), s32[]{:S(2)}) async-start(), calls=%async_computation.3 | async-start | bytes 5898240 | tf_op jit(solution)/shard_map/all_gather | solution.py:16
  156.1 1.8 copy-start.21
  157.0 0.9 copy-start.9
  159.8 333.1 %reduce-scatter.7.cloned.1.call-start = ((), (), s32[]{:S(2)}) async-start(), calls=%async_computation.5 | async-start | bytes 14745600
  180.7 1.1 copy-start.4
  180.8 2.4 copy-start.3
  180.8 2.4 copy-start.18
  183.1 1.1 copy-start.8
  183.1 1.3 copy-start.10
  183.1 1.3 copy-start.13
  183.2 1.3 copy-start.24
  183.2 1.3 copy-start.26
  183.2 1.3 copy-start.27
  275.8 0.7 copy-start.20
  276.5 3.6 copy-start.11
  276.5 3.6 copy-start.14
  281.7 211.1 %copy-start.1 = (bf16[256,2560]{1,0:T(8,128)(2,1)S(1)}, bf16[256,2560]{1,0:T(8,128)(2,1)}, u32[]{:S(2)}) copy-start(bf16[256,2560]{1,0:T(8,128)(2,1)} %param.11) | copy-start | bytes 3932164
  282.8 1.9 copy-start.28
  282.8 1.9 copy-start.29
  282.8 2.2 copy-start.30
Sparse Core Ops, SparseCore 0:
  13.5 88.9 all-gather.7
  154.4 31.9 reduce-scatter.4
  189.4 86.2 all-gather.5
  280.2 212.6 reduce-scatter.6
where the time goes:
time: 501 us; the launch traced here: 499 us
  waiting for transfers between devices  357 us (71%)
  matrix products  40.3 us (8%)
  local copies, waits for them, and re-layouts  39.7 us (8%)
  other arithmetic  25.7 us (5%)
  blocking collectives  22.4 us (4%)
  between operations  14.1 us (3%)
    unnamed x5, waiting for transfers between devices  207 us
    all_gather x2, waiting for transfers between devices, carried_in(): gathered = jax.tree.map(lambda a: lax.all_gather(a, axis), part)  150 us
    all_gather x1, blocking collectives, carried_in(): gathered = jax.tree.map(lambda a: lax.all_gather(a, axis), part)  22.4 us
    unnamed x65, local copies, waits for them, and re-layouts  19.7 us
    add x7, other arithmetic, combine_pairs(): second_part[0][:, None, None] * first_part[1] + second_part[1]  18 us
    dynamic_slice x14, local copies, waits for them, and re-layouts, one(): lax.dynamic_index_in_dim(a, source, 0, False)  10.7 us
  transfers between devices with their start and end apart: 4, of which 3 were waited for; matrix products, arithmetic and copies ran while one was open for 9% of the time, Pallas kernels for 0%

commit v1 on v0

v1 whole, which is shorter than its diff:
```python
import functools

import jax
import jax.numpy as jnp
from jax import lax
from jax.experimental import pallas as pl
from jax.experimental.pallas import tpu as pltpu
from jax.sharding import PartitionSpec as P

SPAN = 256
LANES = 128
MESH = pl.DeviceIdType.MESH
highest = lax.Precision.HIGHEST
f32 = jnp.float32
bf16 = jnp.bfloat16


def dot_f32(a, b, dims=(((1,), (0,)), ((), ()))):
    return lax.dot_general(a, b, dims, preferred_element_type=f32)


def dot_exact(a, b, dims=(((1,), (0,)), ((), ()))):
    return lax.dot_general(a, b, dims, preferred_element_type=f32, precision=highest)


ROWS = (((0,), (0,)), ((), ()))
COLS = (((1,), (1,)), ((), ()))


def split_two(a):
    high = a.astype(bf16)
    return high, (a - high.astype(f32)).astype(bf16)


def span_kernel(n, swap, *refs):
    tok, xw, b_ref, c_ref, ld, st, cot = refs[:7]
    refs = refs[7:]
    if swap:
        tsend, refs = refs[0], refs[1:]
    y_ref, pg_ref, dg_ref = refs[:3]
    refs = refs[3:]
    if swap:
        trecv, refs = refs[0], refs[1:]
    (x_s, pre_s, ce_s, st_s, cum_t, inner_s, back_s, score_s, loc_f, loc_b, out_f, out_b,
     prior, adj, q1_s, q2_s, th_s, send_f, recv_f, send_b, recv_b, tsend_sem, trecv_sem) = refs
    d = lax.axis_index("seq")
    rows, width = cot.shape
    heads = ld.shape[1]
    hdim = width // heads
    pairs = width // LANES
    per = LANES // hdim

    barrier = pltpu.get_barrier_semaphore()
    if swap:
        for o in range(1, n):
            pl.semaphore_signal(barrier, 1, device_id={"seq": lax.rem(d + o, n)}, device_id_type=MESH)
        pl.semaphore_wait(barrier, n - 1)
    else:
        for o in (1, n - 1):
            pl.semaphore_signal(barrier, 1, device_id={"seq": lax.rem(d + o, n)}, device_id_type=MESH)
        pl.semaphore_wait(barrier, 2)

    def tcopy(o):
        to = lax.rem(d + o, n)
        return pltpu.make_async_remote_copy(
            src_ref=tsend.at[to], dst_ref=trecv.at[o], send_sem=tsend_sem.at[o],
            recv_sem=trecv_sem.at[o], device_id={"seq": to}, device_id_type=MESH)

    if swap:
        trecv[0] = tsend[d]
        for o in range(1, n):
            tcopy(o).start()

    row_ids = lax.broadcasted_iota(jnp.int32, (rows, rows), 0)
    col_ids = lax.broadcasted_iota(jnp.int32, (rows, rows), 1)
    lower = row_ids >= col_ids
    lower_ones = lower.astype(f32)
    decay = ld[...]
    cum = dot_exact(lower_ones, decay)
    cum_t[...] = dot_exact(decay, lower_ones, (((0,), (1,)), ((), ())))
    spread = (lax.broadcasted_iota(jnp.int32, (heads, width), 0)
              == lax.broadcasted_iota(jnp.int32, (heads, width), 1) // hdim).astype(f32)
    wide_cum = dot_exact(cum, spread)
    wide_step = dot_exact(st[...], spread)
    for p in range(pairs):
        ce_s[p] = wide_cum[:, p * LANES:(p + 1) * LANES]
        st_s[p] = wide_step[:, p * LANES:(p + 1) * LANES]
    b_val, c_val = b_ref[...], c_ref[...]
    score_s[...] = jnp.where(lower, dot_f32(c_val, b_val, COLS), 0.0)

    step_cols = 2 * LANES
    for k in range(width // step_cols):
        cols = slice(k * step_cols, (k + 1) * step_cols)
        ce = wide_cum[:, cols]
        gw = (cot[:, cols].astype(f32) * jnp.exp(ce)).astype(bf16)
        grad_k = dot_f32(c_val, gw, ROWS)
        pre = dot_f32(tok[...], xw[:, cols])
        act = pre / (1.0 + jnp.exp(-pre))
        xk = (act * wide_step[:, cols]).astype(bf16)
        xwk = (xk.astype(f32) * jnp.exp(ce[rows - 1:rows] - ce)).astype(bf16)
        state_k = dot_f32(b_val, xwk, ROWS)
        for i in range(2):
            half = slice(i * LANES, (i + 1) * LANES)
            pre_s[2 * k + i] = pre[:, half]
            x_s[2 * k + i] = xk[:, half]
            loc_b[2 * k + i] = grad_k[:, half]
            loc_f[2 * k + i] = state_k[:, half]

    @pl.when(d == 0)
    def _():
        prior[...] = jnp.zeros_like(prior)

    @pl.when(d == n - 1)
    def _():
        adj[...] = jnp.zeros_like(adj)

    def fcopy(k):
        return pltpu.make_async_remote_copy(
            src_ref=out_f.at[k], dst_ref=prior.at[k], send_sem=send_f.at[k], recv_sem=recv_f.at[k],
            device_id={"seq": lax.rem(d + 1, n)}, device_id_type=MESH)

    def bcopy(k):
        return pltpu.make_async_remote_copy(
            src_ref=out_b.at[k], dst_ref=adj.at[k], send_sem=send_b.at[k], recv_sem=recv_b.at[k],
            device_id={"seq": lax.rem(d + n - 1, n)}, device_id_type=MESH)

    lane = lax.broadcasted_iota(jnp.int32, (rows, LANES), 1)

    def mix(p):
        ce = ce_s[p]
        xp = x_s[p]
        gp = cot[:, pl.ds(pl.multiple_of(p * LANES, LANES), LANES)]
        inner = back = None
        for i in range(per):
            gap = ce[:, i * hdim:i * hdim + 1] - cum_t[pl.ds(per * p + i, 1), :]
            m = (score_s[...] * jnp.exp(jnp.minimum(gap, 0.0))).astype(bf16)
            inner_i = dot_f32(m, xp)
            back_i = dot_f32(m, gp, ROWS)
            if inner is None:
                inner, back = inner_i, back_i
            else:
                inner = jnp.where(lane < i * hdim, inner, inner_i)
                back = jnp.where(lane < i * hdim, back, back_i)
        inner_s[p] = inner
        back_s[p] = back

    def chain(s, carry):
        kf = s - d

        @pl.when(jnp.logical_and(kf >= 0, kf < pairs))
        def _():
            @pl.when(d > 0)
            def _():
                fcopy(kf).wait_recv()

            @pl.when(d < n - 1)
            def _():
                out_f[kf] = jnp.exp(ce_s[kf, rows - 1:rows, :]) * prior[kf] + loc_f[kf]
                fcopy(kf).start()

        kb = s - (n - 1 - d)

        @pl.when(jnp.logical_and(kb >= 0, kb < pairs))
        def _():
            @pl.when(d < n - 1)
            def _():
                bcopy(kb).wait_recv()

            @pl.when(d > 0)
            def _():
                out_b[kb] = jnp.exp(ce_s[kb, rows - 1:rows, :]) * adj[kb] + loc_b[kb]
                bcopy(kb).start()

        @pl.when(s < pairs)
        def _():
            mix(s)

        return carry

    lax.fori_loop(0, n - 1 + pairs, chain, 0)

    q1_s[...] = jnp.zeros_like(q1_s)
    q2_s[...] = jnp.zeros_like(q2_s)
    th_s[...] = jnp.zeros_like(th_s)

    def finish(p, carry):
        ce = ce_s[p]
        end = ce[rows - 1:rows]
        at = pl.ds(pl.multiple_of(p * LANES, LANES), LANES)
        grad = cot[:, at].astype(f32)
        x = x_s[p].astype(f32)
        pr, ad = prior[p], adj[p]
        hi, lo = split_two(pr)
        y = inner_s[p] + jnp.exp(ce) * (dot_f32(c_val, hi) + dot_f32(c_val, lo))
        y_ref[:, at] = y.astype(bf16)
        hi, lo = split_two(ad)
        bc = jnp.exp(end - ce) * (dot_f32(b_val, hi) + dot_f32(b_val, lo))
        bi = back_s[p]
        pre = pre_s[p]
        sig = 1.0 / (1.0 + jnp.exp(-pre))
        pg = (bi + bc) * st_s[p] * sig * (1.0 + pre * (1.0 - sig))
        pg_ref[:, at] = pg.astype(bf16).astype(f32)
        pick = (lax.broadcasted_iota(jnp.int32, (LANES, heads), 0) // hdim + per * p
                == lax.broadcasted_iota(jnp.int32, (LANES, heads), 1)).astype(f32)
        q1_s[...] += dot_exact(grad * y - x * bi, pick)
        q2_s[...] += dot_exact(x * bc, pick)
        through = jnp.exp(end) * jnp.sum(pr * ad, axis=0, keepdims=True)
        th_s[...] += dot_exact(jnp.broadcast_to(through, (8, LANES)), pick)
        return carry

    lax.fori_loop(0, pairs, finish, 0)
    strict_ones = (row_ids > col_ids).astype(f32)
    dg_ref[...] = (dot_exact(lower_ones, q1_s[...], ROWS) + dot_exact(strict_ones, q2_s[...])
                   + th_s[0:1, :])

    @pl.when(d < n - 1)
    def _():
        def one(k, carry):
            fcopy(k).wait_send()
            return carry
        lax.fori_loop(0, pairs, one, 0)

    @pl.when(d > 0)
    def _():
        def one(k, carry):
            bcopy(k).wait_send()
            return carry
        lax.fori_loop(0, pairs, one, 0)

    if swap:
        for o in range(1, n):
            tcopy(o).wait()


def span_call(n, swap, *args):
    tokens, x_weight, b_input, _, log_decay, _, cotangent = args[:7]
    rows, width = cotangent.shape
    heads, state = log_decay.shape[1], b_input.shape[1]
    pairs = width // LANES
    vm = pl.BlockSpec(memory_space=pltpu.VMEM)
    outs = [jax.ShapeDtypeStruct((rows, width), bf16), jax.ShapeDtypeStruct((rows, width), f32),
            jax.ShapeDtypeStruct((rows, heads), f32)]
    if swap:
        outs.append(jax.ShapeDtypeStruct(args[7].shape, f32))
    wide = pltpu.VMEM((pairs, rows, LANES), f32)
    states = pltpu.VMEM((pairs, state, LANES), f32)
    dma = pltpu.SemaphoreType.DMA
    flops = 2 * rows * tokens.shape[1] * width
    return pl.pallas_call(
        functools.partial(span_kernel, n, swap),
        out_shape=outs,
        in_specs=[vm] * len(args),
        out_specs=[vm] * len(outs),
        scratch_shapes=[
            pltpu.VMEM((pairs, rows, LANES), bf16), wide, wide, wide, pltpu.VMEM((heads, rows), f32),
            wide, wide, pltpu.VMEM((rows, rows), f32), states, states, states, states, states, states,
            pltpu.VMEM((rows, heads), f32), pltpu.VMEM((rows, heads), f32), pltpu.VMEM((8, heads), f32),
            dma((pairs,)), dma((pairs,)), dma((pairs,)), dma((pairs,)), dma((n,)), dma((n,))],
        compiler_params=pltpu.CompilerParams(
            collective_id=0, has_side_effects=True, vmem_limit_bytes=56 << 20),
        cost_estimate=pl.CostEstimate(flops=flops, bytes_accessed=12 << 20, transcendentals=1 << 20),
        name="span",
    )(*args)


def ring_kernel(n, nh, pg, xw, tq, wg_ref, tg_ref, gat, tokall, part, got, send, recv, tok_send,
                tok_recv, g_send, g_recv):
    d, h = lax.axis_index("seq"), lax.axis_index("head")
    rows, width = pg.shape
    quarter = rows // nh
    tcols = tg_ref.shape[1]
    side = lax.rem(d, 2)
    pos = jnp.where(side == 0, d // 2, n - 1 - d // 2)

    def member(p):
        return jnp.where(p < n // 2, 2 * p, 2 * (n - 1 - p) + 1)

    right, left = member(lax.rem(pos + 1, n)), member(lax.rem(pos + n - 1, n))
    barrier = pltpu.get_barrier_semaphore()
    for to in (right, left):
        pl.semaphore_signal(barrier, 1, device_id={"seq": to}, device_id_type=MESH)
    for o in range(1, nh):
        pl.semaphore_signal(barrier, 1, device_id={"head": lax.rem(h + o, nh)}, device_id_type=MESH)
    pl.semaphore_wait(barrier, 1 + nh)

    def hop(j, q, src):
        return pltpu.make_async_remote_copy(
            src_ref=src, dst_ref=gat.at[j, q], send_sem=send.at[j, q], recv_sem=recv.at[j, q],
            device_id={"seq": right if q < nh // 2 else left}, device_id_type=MESH)

    def first(q):
        return hop(0, q, pg.at[pl.ds(q * quarter, quarter), :])

    order = [q for pair in zip(range(nh // 2), range(nh // 2, nh)) for q in pair]
    for q in order:
        first(q).start()

    def tcopy(o):
        return pltpu.make_async_remote_copy(
            src_ref=tq, dst_ref=tokall.at[o], send_sem=tok_send.at[o], recv_sem=tok_recv.at[o],
            device_id={"head": lax.rem(h + o, nh)}, device_id_type=MESH)

    def gcopy(o):
        return pltpu.make_async_remote_copy(
            src_ref=part.at[o], dst_ref=got.at[o], send_sem=g_send.at[o], recv_sem=g_recv.at[o],
            device_id={"head": lax.rem(h + o, nh)}, device_id_type=MESH)

    for o in range(1, nh):
        tcopy(o).start()
    tokall[0] = tq[...]
    pgb = pg[...].astype(bf16)
    for o in list(range(1, nh)) + [0]:
        to = lax.rem(h + o, nh)
        part[o] = dot_f32(pgb, xw[pl.ds(pl.multiple_of(to * tcols, tcols), tcols), :], COLS)
        if o:
            gcopy(o).start()
    for o in range(1, nh):
        tcopy(o).wait()

    def tok_rows(src, quarters):
        off = lax.rem(d - src + n, n)
        return jnp.concatenate(
            [tokall[lax.rem(h - q + nh, nh), off].astype(bf16) for q in quarters], axis=0)

    wg_ref[...] = dot_f32(tok_rows(d, range(nh)), pgb, ROWS)
    halves = (range(nh // 2), range(nh // 2, nh))

    def step(j, carry):
        for q in order:
            hop(j, q, gat.at[j, q]).wait_recv()

            @pl.when(j < n - 2)
            def _():
                hop(j + 1, q, gat.at[j, q]).start()

        sources = (member(lax.rem(pos + n - 1 - j, n)), member(lax.rem(pos + 1 + j, n)))
        total = wg_ref[...]
        for src, quarters in zip(sources, halves):
            block = jnp.concatenate([gat[j, q].astype(bf16) for q in quarters], axis=0)
            total = total + dot_f32(tok_rows(src, quarters), block, ROWS)
        wg_ref[...] = total
        return carry

    lax.fori_loop(0, n - 1, step, 0)
    total = part[0]
    for o in range(1, nh):
        gcopy(o).wait()
        total = total + got[o]
    tg_ref[...] = total.astype(bf16)
    for q in order:
        first(q).wait_send()

    def drain(j, carry):
        for q in order:
            hop(j, q, gat.at[j - 1, q]).wait_send()
        return carry

    lax.fori_loop(1, n - 1, drain, 0)


def ring_call(n, nh, pg, x_weight, tq):
    rows, width = pg.shape
    depth = x_weight.shape[0]
    cols, tcols = tq.shape[2], depth // nh
    vm = pl.BlockSpec(memory_space=pltpu.VMEM)
    dma = pltpu.SemaphoreType.DMA
    return pl.pallas_call(
        functools.partial(ring_kernel, n, nh),
        out_shape=[jax.ShapeDtypeStruct((cols, width), f32), jax.ShapeDtypeStruct((rows, tcols), bf16)],
        in_specs=[vm] * 3,
        out_specs=[vm] * 2,
        scratch_shapes=[
            pltpu.VMEM((n - 1, nh, rows // nh, width), f32), pltpu.VMEM((nh,) + tq.shape, f32),
            pltpu.VMEM((nh, rows, tcols), f32), pltpu.VMEM((nh, rows, tcols), f32),
            dma((n - 1, nh)), dma((n - 1, nh)), dma((nh,)), dma((nh,)), dma((nh,)), dma((nh,))],
        compiler_params=pltpu.CompilerParams(
            collective_id=1, has_side_effects=True, vmem_limit_bytes=56 << 20),
        cost_estimate=pl.CostEstimate(
            flops=4 * rows * depth * width, bytes_accessed=12 << 20, transcendentals=0),
        name="ring",
    )(pg, x_weight, tq)


def per_device(tokens, x_weight, b_input, c_input, log_decay, step_size, cotangent):
    n, nh = lax.axis_size("seq"), lax.axis_size("head")
    rows, depth = tokens.shape
    assert rows == SPAN and n % 2 == 0
    swap = 4 <= n <= 16
    args = (tokens, x_weight, b_input, c_input, log_decay, step_size, cotangent)
    if swap:
        quarter = rows // nh
        mine = lax.dynamic_slice_in_dim(tokens, lax.axis_index("head") * quarter, quarter, 0)
        mine = jnp.transpose(mine.reshape(quarter, n, depth // n), (1, 0, 2)).astype(f32)
        y, pg, dg, tq = span_call(n, True, *args, mine)
        wg, tg = ring_call(n, nh, pg, x_weight, tq)
        return y, tg, wg, dg
    y, pg, dg = span_call(n, False, *args)
    pgb = pg.astype(bf16)
    wg = lax.psum_scatter(dot_f32(tokens, pgb, ROWS), "seq", scatter_dimension=0, tiled=True)
    tg = lax.psum_scatter(dot_f32(pgb, x_weight, COLS), "head", scatter_dimension=1, tiled=True)
    return y, tg.astype(bf16), wg, dg


def solution(mesh):
    return jax.shard_map(
        per_device,
        mesh=mesh,
        in_specs=(
            P("seq", None),
            P(None, "head"),
            P("seq", None),
            P("seq", None),
            P("seq", "head"),
            P("seq", "head"),
            P("seq", "head"),
        ),
        out_specs=(P("seq", "head"), P("seq", "head"), P("seq", "head"), P("seq", "head")),
        check_vma=False,
    )
```

time: 501 us -> 228 us (0.46)
  waiting for transfers between devices: 357 us -> 0 us
  Pallas kernels: 0 us -> 215 us
  matrix products: 40.3 us -> 0 us
  local copies, waits for them, and re-layouts: 39.7 us -> 9.58 us
  other arithmetic: 25.7 us -> 1.02 us
  blocking collectives: 22.4 us -> 0 us
  between operations: 14.1 us -> 0.68 us
    pallas_call x0 -> x2, Pallas kernels: none -> 215 us  [the longest x1 128 us: ring_call(): pl.pallas_call(functools.partial(ring_kernel, n, nh), out_shape=[jax.Shap...]
    unnamed x5 -> x0, waiting for transfers between devices: 207 us -> none
    all_gather x2 -> x0, waiting for transfers between devices: 150 us -> none  [carried_in(): gathered = jax.tree.map(lambda a: lax.all_gather(a, axis), part)]
    dot_general x14 -> x0, matrix products: 40.3 us -> none  [the longest x1 6.68 us: weight_rows(): lax.dot_general(inputs, gradients, (((0,), (0,)), ((), ())), preferred_el...]
    all_gather x1 -> x0, blocking collectives: 22.4 us -> none  [carried_in(): gathered = jax.tree.map(lambda a: lax.all_gather(a, axis), part)]
    add x7 -> x0, other arithmetic: 18 us -> none  [combine_pairs(): second_part[0][:, None, None] * first_part[1] + second_part[1]]
    unnamed x65 -> x10, local copies, waits for them, and re-layouts: 19.7 us -> 8.33 us
    dynamic_slice x14 -> x0, local copies, waits for them, and re-layouts: 10.7 us -> none  [one(): lax.dynamic_index_in_dim(a, source, 0, False)]
  transfers between devices with their start and end apart: 4 -> 0, of which waited for: 3 -> 0; matrix products, arithmetic and copies ran while one was open for 9% -> 0% of each run, Pallas kernels for 0% -> 0%
where the time goes in v1:
time: 228 us; the launch traced here: 227 us
  Pallas kernels  215 us (94%)
  local copies, waits for them, and re-layouts  9.58 us (4%)
    pallas_call x1, Pallas kernels, ring_call(): pl.pallas_call(functools.partial(ring_kernel, n, nh), out_shape=[jax.Shap...  128 us
    pallas_call x1, Pallas kernels, span_call(): pl.pallas_call(functools.partial(span_kernel, n, swap), out_shape=outs, i...  87.5 us
    unnamed x10, local copies, waits for them, and re-layouts  8.33 us

profile of v1, /device:TPU:0, one launch (start us, length us, event | category | flops | bytes accessed | tf_op | source)
XLA Modules:
  0.0 226.8 jit_solution(16174841550049531618)
XLA Ops:
  0.6 1.5 copy.15.refs_4_
  2.1 1.5 copy.16.refs_5_
  3.6 1.0 dynamic-slice_convert_fusion
  4.7 0.2 reshape.11
  4.9 1.0 copy.19
  5.9 87.5 %span.1 = (bf16[256,1280]{1,0:T(8,128)(2,1)}, f32[256,1280]{1,0:T(8,128)}, f32[256,20]{1,0:T(8,128)}, f32[8,64,320]{2,1,0:T(8,128)}) custom-call(bf16[256,2560]{1,0:T(8,128)(2,1)} %refs_0_.1, bf16[2560,1280]{1,0:T(8,128)(2,1)} %xw.1, bf16[256,128]{1,0:T(8,128)(2,1)} %refs_2_.1, bf16[256,128]{1,0:T(8,128)(2,1)} %refs_3_.1, f32[256,20]{1,0:T(8,128)} %copy.15.refs_4_, ...), custom_call_target="tpu_custom_call" | custom-call | flops 1677721600 | bytes 12582912 | tf_op jit(solution)/shard_map/span/pallas_call | solution.py:249
  93.5 1.6 copy.17
  95.1 0.0 copy-start.1
  95.1 127.9 %ring.1 = (f32[320,1280]{1,0:T(8,128)}, bf16[256,640]{1,0:T(8,128)(2,1)}) custom-call(f32[256,1280]{1,0:T(8,128)} %get-tuple-element.11.pg, bf16[2560,1280]{1,0:T(8,128)(2,1)} %xw.1, f32[8,64,320]{2,1,0:T(8,128)} %get-tuple-element.12.tq), custom_call_target="tpu_custom_call" | custom-call | flops 3355443200 | bytes 12582912 | tf_op jit(solution)/shard_map/ring/pallas_call | solution.py:367
  223.0 0.0 copy-start
  223.0 0.0 copy-done.1
  223.0 0.8 copy.23
  223.9 1.7 copy.24
  225.6 0.0 copy-done
  225.6 1.2 copy.25
Async XLA Ops:
  95.1 128.0 %copy-start.1 = (bf16[256,1280]{1,0:T(8,128)(2,1)S(1)}, bf16[256,1280]{1,0:T(8,128)(2,1)}, u32[]{:S(2)}) copy-start(bf16[256,1280]{1,0:T(8,128)(2,1)} %get-tuple-element.28) | copy-start | bytes 1966084
  223.0 2.6 %copy-start = (f32[320,1280]{1,0:T(8,128)S(1)}, f32[320,1280]{1,0:T(8,128)}, u32[]{:S(2)}) copy-start(f32[320,1280]{1,0:T(8,128)} %get-tuple-element.30) | copy-start | bytes 4915204

commit v2 on v1

v2 whole, which is shorter than its diff:
```python
import functools

import jax
import jax.numpy as jnp
from jax import lax
from jax.experimental import pallas as pl
from jax.experimental.pallas import tpu as pltpu
from jax.sharding import PartitionSpec as P

SPAN = 256
LANES = 128
MESH = pl.DeviceIdType.MESH
highest = lax.Precision.HIGHEST
f32 = jnp.float32
bf16 = jnp.bfloat16


def dot_f32(a, b, dims=(((1,), (0,)), ((), ()))):
    return lax.dot_general(a, b, dims, preferred_element_type=f32)


def dot_exact(a, b, dims=(((1,), (0,)), ((), ()))):
    return lax.dot_general(a, b, dims, preferred_element_type=f32, precision=highest)


ROWS = (((0,), (0,)), ((), ()))
COLS = (((1,), (1,)), ((), ()))


def split_two(a):
    high = a.astype(bf16)
    return high, (a - high.astype(f32)).astype(bf16)


def span_kernel(n, nh, ring, *refs):
    tok, xw, b_ref, c_ref, ld, st, cot = refs[:7]
    refs = refs[7:]
    if ring:
        tsend, y_ref, dg_ref, wg_ref, tg_ref = refs[:5]
        refs = refs[5:]
    else:
        y_ref, pg_ref, dg_ref = refs[:3]
        refs = refs[3:]
    (x_s, pre_s, ce_s, st_s, cum_t, inner_s, back_s, score_s, loc_f, loc_b, out_f, out_b,
     prior, adj, q1_s, q2_s, th_s, send_f, recv_f, send_b, recv_b) = refs[:21]
    if ring:
        (pg_s, gat, tokall, tokmat, part, got, r_send, r_recv, t_send, t_recv, h_send, h_recv,
         g_send, g_recv) = refs[21:]
    d, h = lax.axis_index("seq"), lax.axis_index("head")
    rows, width = cot.shape
    heads = ld.shape[1]
    hdim = width // heads
    pairs = width // LANES
    per = LANES // hdim
    quarter, half = rows // nh, rows // 2

    barrier = pltpu.get_barrier_semaphore()
    for o in range(1, n) if ring else (1, n - 1):
        pl.semaphore_signal(barrier, 1, device_id={"seq": lax.rem(d + o, n)}, device_id_type=MESH)
    if ring:
        for o in range(1, nh):
            pl.semaphore_signal(barrier, 1, device_id={"head": lax.rem(h + o, nh)}, device_id_type=MESH)
    pl.semaphore_wait(barrier, n + nh - 2 if ring else 2)

    if ring:
        side = lax.rem(d, 2)
        pos = jnp.where(side == 0, d // 2, n - 1 - d // 2)

        def member(p):
            return jnp.where(p < n // 2, 2 * p, 2 * (n - 1 - p) + 1)

        next_to = (member(lax.rem(pos + 1, n)), member(lax.rem(pos + n - 1, n)))

        def tcopy(o):
            to = lax.rem(d + o, n)
            return pltpu.make_async_remote_copy(
                src_ref=tsend.at[to], dst_ref=tokall.at[0, o], send_sem=t_send.at[o],
                recv_sem=t_recv.at[o], device_id={"seq": to}, device_id_type=MESH)

        def hcopy(o):
            return pltpu.make_async_remote_copy(
                src_ref=tokall.at[0], dst_ref=tokall.at[o], send_sem=h_send.at[o],
                recv_sem=h_recv.at[o], device_id={"head": lax.rem(h + o, nh)}, device_id_type=MESH)

        def gcopy(o):
            return pltpu.make_async_remote_copy(
                src_ref=part.at[o], dst_ref=got.at[o], send_sem=g_send.at[o], recv_sem=g_recv.at[o],
                device_id={"head": lax.rem(h + o, nh)}, device_id_type=MESH)

        def hop(j, k, w, src):
            return pltpu.make_async_remote_copy(
                src_ref=src, dst_ref=gat.at[j, k, w], send_sem=r_send.at[j, k, w],
                recv_sem=r_recv.at[j, k, w], device_id={"seq": next_to[w]}, device_id_type=MESH)

        tokall[0, 0] = tsend[d]
        for o in range(1, n):
            tcopy(o).start()

    row_ids = lax.broadcasted_iota(jnp.int32, (rows, rows), 0)
    col_ids = lax.broadcasted_iota(jnp.int32, (rows, rows), 1)
    lower = row_ids >= col_ids
    lower_ones = lower.astype(f32)
    decay = ld[...]
    cum = dot_exact(lower_ones, decay)
    cum_t[...] = dot_exact(decay, lower_ones, (((0,), (1,)), ((), ())))
    spread = (lax.broadcasted_iota(jnp.int32, (heads, width), 0)
              == lax.broadcasted_iota(jnp.int32, (heads, width), 1) // hdim).astype(f32)
    wide_cum = dot_exact(cum, spread)
    wide_step = dot_exact(st[...], spread)
    for p in range(pairs):
        ce_s[p] = wide_cum[:, p * LANES:(p + 1) * LANES]
        st_s[p] = wide_step[:, p * LANES:(p + 1) * LANES]
    b_val, c_val = b_ref[...], c_ref[...]
    score_s[...] = jnp.where(lower, dot_f32(c_val, b_val, COLS), 0.0)
    q1_s[...] = jnp.zeros_like(q1_s)
    q2_s[...] = jnp.zeros_like(q2_s)
    th_s[...] = jnp.zeros_like(th_s)

    step_cols = 2 * LANES
    for k in range(width // step_cols):
        cols = slice(k * step_cols, (k + 1) * step_cols)
        ce = wide_cum[:, cols]
        gw = (cot[:, cols].astype(f32) * jnp.exp(ce)).astype(bf16)
        grad_k = dot_f32(c_val, gw, ROWS)
        pre = dot_f32(tok[...], xw[:, cols])
        act = pre / (1.0 + jnp.exp(-pre))
        xk = (act * wide_step[:, cols]).astype(bf16)
        xwk = (xk.astype(f32) * jnp.exp(ce[rows - 1:rows] - ce)).astype(bf16)
        state_k = dot_f32(b_val, xwk, ROWS)
        for i in range(2):
            at = slice(i * LANES, (i + 1) * LANES)
            pre_s[2 * k + i] = pre[:, at]
            x_s[2 * k + i] = xk[:, at]
            loc_b[2 * k + i] = grad_k[:, at]
            loc_f[2 * k + i] = state_k[:, at]

    @pl.when(d == 0)
    def _():
        prior[...] = jnp.zeros_like(prior)

    @pl.when(d == n - 1)
    def _():
        adj[...] = jnp.zeros_like(adj)

    def fcopy(k):
        return pltpu.make_async_remote_copy(
            src_ref=out_f.at[k], dst_ref=prior.at[k], send_sem=send_f.at[k], recv_sem=recv_f.at[k],
            device_id={"seq": lax.rem(d + 1, n)}, device_id_type=MESH)

    def bcopy(k):
        return pltpu.make_async_remote_copy(
            src_ref=out_b.at[k], dst_ref=adj.at[k], send_sem=send_b.at[k], recv_sem=recv_b.at[k],
            device_id={"seq": lax.rem(d + n - 1, n)}, device_id_type=MESH)

    lane = lax.broadcasted_iota(jnp.int32, (rows, LANES), 1)

    def mix(p):
        ce = ce_s[p]
        xp = x_s[p]
        gp = cot[:, pl.ds(pl.multiple_of(p * LANES, LANES), LANES)]
        inner = back = None
        for i in range(per):
            gap = ce[:, i * hdim:i * hdim + 1] - cum_t[pl.ds(per * p + i, 1), :]
            m = (score_s[...] * jnp.exp(jnp.minimum(gap, 0.0))).astype(bf16)
            inner_i = dot_f32(m, xp)
            back_i = dot_f32(m, gp, ROWS)
            if inner is None:
                inner, back = inner_i, back_i
            else:
                inner = jnp.where(lane < i * hdim, inner, inner_i)
                back = jnp.where(lane < i * hdim, back, back_i)
        inner_s[p] = inner
        back_s[p] = back

    def finish(p):
        ce = ce_s[p]
        end = ce[rows - 1:rows]
        at = pl.ds(pl.multiple_of(p * LANES, LANES), LANES)
        pr, ad = prior[p], adj[p]
        hi, lo = split_two(ad)
        bc = jnp.exp(end - ce) * (dot_f32(b_val, hi) + dot_f32(b_val, lo))
        bi = back_s[p]
        pre = pre_s[p]
        sig = 1.0 / (1.0 + jnp.exp(-pre))
        pg = (bi + bc) * st_s[p] * sig * (1.0 + pre * (1.0 - sig))
        pg = pg.astype(bf16).astype(f32)
        if ring:
            pg_s[p, 0] = pg[:half]
            pg_s[p, 1] = pg[half:]
            for w in range(2):
                hop(0, p, w, pg_s.at[p, w]).start()
        else:
            pg_ref[:, at] = pg
        grad = cot[:, at].astype(f32)
        x = x_s[p].astype(f32)
        hi, lo = split_two(pr)
        y = inner_s[p] + jnp.exp(ce) * (dot_f32(c_val, hi) + dot_f32(c_val, lo))
        y_ref[:, at] = y.astype(bf16)
        pick = (lax.broadcasted_iota(jnp.int32, (LANES, heads), 0) // hdim + per * p
                == lax.broadcasted_iota(jnp.int32, (LANES, heads), 1)).astype(f32)
        q1_s[...] += dot_exact(grad * y - x * bi, pick)
        q2_s[...] += dot_exact(x * bc, pick)
        through = jnp.exp(end) * jnp.sum(pr * ad, axis=0, keepdims=True)
        th_s[...] += dot_exact(jnp.broadcast_to(through, (8, LANES)), pick)

    def forward(s):
        def one(k, carry):
            j = s - n - k

            @pl.when(jnp.logical_and(j >= 0, j < n - 1))
            def _():
                for w in range(2):
                    hop(j, k, w, gat.at[j, k, w]).wait_recv()

                    @pl.when(j < n - 2)
                    def _():
                        hop(j + 1, k, w, gat.at[j, k, w]).start()

            return carry

        lax.fori_loop(0, pairs, one, 0)

    def arrange():
        for o in range(1, nh):
            hcopy(o).wait()

        def place(slot, src, q):
            tokmat[slot, q * quarter:(q + 1) * quarter, :] = tokall[
                lax.rem(h - q + nh, nh), lax.rem(d - src + n, n)].astype(bf16)

        def one(slot, carry):
            for q in range(nh):
                p = pos + n - slot if q < nh // 2 else pos + slot
                place(slot, member(lax.rem(p, n)), q)
            return carry

        lax.fori_loop(0, n, one, 0)

    def weights(k):
        blocks = [jnp.concatenate([pg_s[k + i, w] for i in range(2)], axis=1).astype(bf16)
                  for w in range(2)]
        for j in range(n - 1):
            for w in range(2):
                blocks.append(jnp.concatenate(
                    [gat[j, k + i, w] for i in range(2)], axis=1).astype(bf16))
        wg_ref[:, pl.ds(pl.multiple_of(k * LANES, 2 * LANES), 2 * LANES)] = dot_f32(
            tokmat[...].reshape(n * rows, tokmat.shape[2]), jnp.concatenate(blocks, axis=0), ROWS)

    def input_part(o):
        tcols = part.shape[2]
        to = lax.rem(h + o, nh)
        pgb = jnp.concatenate(
            [jnp.concatenate([pg_s[p, w].astype(bf16) for p in range(pairs)], axis=1)
             for w in range(2)], axis=0)
        part[o] = dot_f32(pgb, xw[pl.ds(pl.multiple_of(to * tcols, tcols), tcols), :], COLS)
        if o:
            gcopy(o).start()

    def chain(s, carry):
        if ring:
            forward(s)
        kf = s - d

        @pl.when(jnp.logical_and(kf >= 0, kf < pairs))
        def _():
            @pl.when(d > 0)
            def _():
                fcopy(kf).wait_recv()

            @pl.when(d < n - 1)
            def _():
                out_f[kf] = jnp.exp(ce_s[kf, rows - 1:rows, :]) * prior[kf] + loc_f[kf]
                fcopy(kf).start()

        kb = s - (n - 1 - d)

        @pl.when(jnp.logical_and(kb >= 0, kb < pairs))
        def _():
            @pl.when(d < n - 1)
            def _():
                bcopy(kb).wait_recv()

            @pl.when(d > 0)
            def _():
                out_b[kb] = jnp.exp(ce_s[kb, rows - 1:rows, :]) * adj[kb] + loc_b[kb]
                bcopy(kb).start()

        @pl.when(s < pairs)
        def _():
            mix(s)

        ks = s - (n - 1)

        @pl.when(jnp.logical_and(ks >= 0, ks < pairs))
        def _():
            finish(ks)

        if ring:
            @pl.when(s == n - 2)
            def _():
                for o in range(1, n):
                    tcopy(o).wait()
                for o in range(1, nh):
                    hcopy(o).start()

            for o in range(nh):
                @pl.when(s == n - 1 + pairs + (o - 1) % nh)
                def _():
                    input_part(o)

            @pl.when(s == max(2 * n - 2, n + pairs + nh))
            def _():
                arrange()
        return carry

    total_steps = n - 1 + pairs + (n - 1 if ring else 0)
    lax.fori_loop(0, total_steps, chain, 0)

    strict_ones = (row_ids > col_ids).astype(f32)
    dg_ref[...] = (dot_exact(lower_ones, q1_s[...], ROWS) + dot_exact(strict_ones, q2_s[...])
                   + th_s[0:1, :])

    @pl.when(d < n - 1)
    def _():
        def one(k, carry):
            fcopy(k).wait_send()
            return carry
        lax.fori_loop(0, pairs, one, 0)

    @pl.when(d > 0)
    def _():
        def one(k, carry):
            bcopy(k).wait_send()
            return carry
        lax.fori_loop(0, pairs, one, 0)

    if ring:
        def each(k, carry):
            weights(2 * k)
            return carry

        lax.fori_loop(0, pairs // 2, each, 0)
        total = part[0]
        for o in range(1, nh):
            gcopy(o).wait()
            total = total + got[o]
        tg_ref[...] = total.astype(bf16)

        def drain(k, carry):
            for w in range(2):
                hop(0, k, w, pg_s.at[k, w]).wait_send()

                def one(j, carry):
                    hop(j, k, w, gat.at[j - 1, k, w]).wait_send()
                    return carry

                lax.fori_loop(1, n - 1, one, 0)
            return carry

        lax.fori_loop(0, pairs, drain, 0)


def span_call(n, nh, ring, *args):
    tokens, x_weight, b_input, _, log_decay, _, cotangent = args[:7]
    rows, width = cotangent.shape
    depth = tokens.shape[1]
    heads, state = log_decay.shape[1], b_input.shape[1]
    pairs = width // LANES
    vm = pl.BlockSpec(memory_space=pltpu.VMEM)
    wide = pltpu.VMEM((pairs, rows, LANES), f32)
    states = pltpu.VMEM((pairs, state, LANES), f32)
    dma = pltpu.SemaphoreType.DMA
    scratch = [
        pltpu.VMEM((pairs, rows, LANES), bf16), wide, wide, wide, pltpu.VMEM((heads, rows), f32),
        wide, wide, pltpu.VMEM((rows, rows), f32), states, states, states, states, states, states,
        pltpu.VMEM((rows, heads), f32), pltpu.VMEM((rows, heads), f32), pltpu.VMEM((8, heads), f32),
        dma((pairs,)), dma((pairs,)), dma((pairs,)), dma((pairs,))]
    y = jax.ShapeDtypeStruct((rows, width), bf16)
    dg = jax.ShapeDtypeStruct((rows, heads), f32)
    if ring:
        cols, tcols = depth // n, depth // nh
        outs = [y, dg, jax.ShapeDtypeStruct((cols, width), f32), jax.ShapeDtypeStruct((rows, tcols), bf16)]
        out_part = pltpu.VMEM((nh, rows, tcols), f32)
        scratch += [
            pltpu.VMEM((pairs, 2, rows // 2, LANES), f32),
            pltpu.VMEM((n - 1, pairs, 2, rows // 2, LANES), f32),
            pltpu.VMEM((nh,) + args[7].shape, f32), pltpu.VMEM((n, rows, cols), bf16), out_part, out_part,
            dma((n - 1, pairs, 2)), dma((n - 1, pairs, 2)), dma((n,)), dma((n,)),
            dma((nh,)), dma((nh,)), dma((nh,)), dma((nh,))]
    else:
        outs = [y, jax.ShapeDtypeStruct((rows, width), f32), dg]
    return pl.pallas_call(
        functools.partial(span_kernel, n, nh, ring),
        out_shape=outs,
        in_specs=[vm] * len(args),
        out_specs=[vm] * len(outs),
        scratch_shapes=scratch,
        compiler_params=pltpu.CompilerParams(
            collective_id=0, has_side_effects=True, vmem_limit_bytes=60 << 20),
        cost_estimate=pl.CostEstimate(
            flops=6 * rows * depth * width, bytes_accessed=12 << 20, transcendentals=1 << 20),
        name="span",
    )(*args)


def per_device(tokens, x_weight, b_input, c_input, log_decay, step_size, cotangent):
    n, nh = lax.axis_size("seq"), lax.axis_size("head")
    rows, depth = tokens.shape
    assert rows == SPAN and n % 2 == 0
    ring = 4 <= n <= 8
    args = (tokens, x_weight, b_input, c_input, log_decay, step_size, cotangent)
    if ring:
        quarter = rows // nh
        mine = lax.dynamic_slice_in_dim(tokens, lax.axis_index("head") * quarter, quarter, 0)
        mine = jnp.transpose(mine.reshape(quarter, n, depth // n), (1, 0, 2)).astype(f32)
        y, dg, wg, tg = span_call(n, nh, True, *args, mine)
        return y, tg, wg, dg
    y, pg, dg = span_call(n, nh, False, *args)
    pgb = pg.astype(bf16)
    wg = lax.psum_scatter(dot_f32(tokens, pgb, ROWS), "seq", scatter_dimension=0, tiled=True)
    tg = lax.psum_scatter(dot_f32(pgb, x_weight, COLS), "head", scatter_dimension=1, tiled=True)
    return y, tg.astype(bf16), wg, dg


def solution(mesh):
    return jax.shard_map(
        per_device,
        mesh=mesh,
        in_specs=(
            P("seq", None),
            P(None, "head"),
            P("seq", None),
            P("seq", None),
            P("seq", "head"),
            P("seq", "head"),
            P("seq", "head"),
        ),
        out_specs=(P("seq", "head"), P("seq", "head"), P("seq", "head"), P("seq", "head")),
        check_vma=False,
    )
```

time: 228 us -> 187 us (0.82)
  Pallas kernels: 215 us -> 174 us
    pallas_call x2 -> x1, Pallas kernels: 215 us -> 174 us  [span_call(): pl.pallas_call(functools.partial(span_kernel, n, nh, ring), out_shape=out...]
    unnamed x10 -> x8, local copies, waits for them, and re-layouts: 8.33 us -> 9.57 us
where the time goes in v2:
time: 187 us; the launch traced here: 186 us
  Pallas kernels  174 us (93%)
  local copies, waits for them, and re-layouts  10.8 us (6%)
    pallas_call x1, Pallas kernels, span_call(): pl.pallas_call(functools.partial(span_kernel, n, nh, ring), out_shape=out...  174 us
    unnamed x8, local copies, waits for them, and re-layouts  9.57 us

profile of v2, /device:TPU:0, one launch (start us, length us, event | category | flops | bytes accessed | tf_op | source)
XLA Modules:
  0.0 186.5 jit_solution(6193414575264703408)
XLA Ops:
  0.6 1.5 copy.15.refs_4_
  2.1 1.5 copy.16.refs_5_
  3.6 1.0 dynamic-slice_convert_fusion
  4.7 0.2 reshape.11
  4.9 1.0 copy.19
  5.9 174.0 %span.1 = (bf16[256,1280]{1,0:T(8,128)(2,1)}, f32[256,20]{1,0:T(8,128)}, f32[320,1280]{1,0:T(8,128)}, bf16[256,640]{1,0:T(8,128)(2,1)}) custom-call(bf16[256,2560]{1,0:T(8,128)(2,1)} %refs_0_.1, bf16[2560,1280]{1,0:T(8,128)(2,1)} %refs_1_.1, bf16[256,128]{1,0:T(8,128)(2,1)} %refs_2_.1, bf16[256,128]{1,0:T(8,128)(2,1)} %refs_3_.1, f32[256,20]{1,0:T(8,128)} %copy.15.refs_4_, ...), custom_call_target="tpu_custom_call" | custom-call | flops 5033164800 | bytes 12582912 | tf_op jit(solution)/shard_map/span/pallas_call | solution.py:392
  179.9 0.0 copy-start
  179.9 1.7 copy.17
  181.6 2.0 %copy.23 = bf16[256,1280]{1,0:T(8,128)(2,1)} copy(bf16[256,1280]{1,0:T(8,128)(2,1)} %get-tuple-element.24) | data formatting | bytes 1310720
  183.6 1.7 copy.24
  185.3 0.0 copy-done
  185.3 1.2 copy.25
Async XLA Ops:
  179.9 5.4 %copy-start = (f32[320,1280]{1,0:T(8,128)S(1)}, f32[320,1280]{1,0:T(8,128)}, u32[]{:S(2)}) copy-start(f32[320,1280]{1,0:T(8,128)} %get-tuple-element.26) | copy-start | bytes 4915204

commit v3 on v2

--- a/solution.py
+++ b/solution.py
@@ -33,26 +33,28 @@
 
 
 def span_kernel(n, nh, ring, *refs):
-    tok, xw, b_ref, c_ref, ld, st, cot = refs[:7]
+    tok, xw_hbm, b_ref, c_ref, ld, st, cot = refs[:7]
     refs = refs[7:]
     if ring:
-        tsend, y_ref, dg_ref, wg_ref, tg_ref = refs[:5]
-        refs = refs[5:]
+        y_ref, dg_ref, wg_ref, tg_ref = refs[:4]
+        refs = refs[4:]
     else:
         y_ref, pg_ref, dg_ref = refs[:3]
         refs = refs[3:]
     (x_s, pre_s, ce_s, st_s, cum_t, inner_s, back_s, score_s, loc_f, loc_b, out_f, out_b,
-     prior, adj, q1_s, q2_s, th_s, send_f, recv_f, send_b, recv_b) = refs[:21]
-    if ring:
-        (pg_s, gat, tokall, tokmat, part, got, r_send, r_recv, t_send, t_recv, h_send, h_recv,
-         g_send, g_recv) = refs[21:]
+     prior, adj, q1_s, q2_s, th_s, xw, xw_sem, send_f, recv_f, send_b, recv_b) = refs[:23]
+    if ring:
+        (pg_s, pg_t, gat, tsend, tokall, tokmat, part, got, r_send, r_recv, t_send, t_recv, h_send, h_recv,
+         g_send, g_recv) = refs[23:]
     d, h = lax.axis_index("seq"), lax.axis_index("head")
     rows, width = cot.shape
-    heads = ld.shape[1]
+    heads = ld.shape[0]
     hdim = width // heads
     pairs = width // LANES
     per = LANES // hdim
     quarter, half = rows // nh, rows // 2
+    load = pltpu.make_async_copy(xw_hbm, xw, xw_sem)
+    load.start()
 
     barrier = pltpu.get_barrier_semaphore()
     for o in range(1, n) if ring else (1, n - 1):
@@ -92,6 +94,10 @@
                 src_ref=src, dst_ref=gat.at[j, k, w], send_sem=r_send.at[j, k, w],
                 recv_sem=r_recv.at[j, k, w], device_id={"seq": next_to[w]}, device_id_type=MESH)
 
+        mine = tok[pl.ds(pl.multiple_of(h * quarter, quarter), quarter), :]
+        tcols = tsend.shape[2]
+        for i in range(n):
+            tsend[i] = mine[:, i * tcols:(i + 1) * tcols].astype(f32)
         tokall[0, 0] = tsend[d]
         for o in range(1, n):
             tcopy(o).start()
@@ -101,12 +107,12 @@
     lower = row_ids >= col_ids
     lower_ones = lower.astype(f32)
     decay = ld[...]
-    cum = dot_exact(lower_ones, decay)
-    cum_t[...] = dot_exact(decay, lower_ones, (((0,), (1,)), ((), ())))
+    cum = dot_exact(lower_ones, decay, COLS)
+    cum_t[...] = dot_exact(decay, lower_ones, COLS)
     spread = (lax.broadcasted_iota(jnp.int32, (heads, width), 0)
               == lax.broadcasted_iota(jnp.int32, (heads, width), 1) // hdim).astype(f32)
     wide_cum = dot_exact(cum, spread)
-    wide_step = dot_exact(st[...], spread)
+    wide_step = dot_exact(st[...], spread, ROWS)
     for p in range(pairs):
         ce_s[p] = wide_cum[:, p * LANES:(p + 1) * LANES]
         st_s[p] = wide_step[:, p * LANES:(p + 1) * LANES]
@@ -116,6 +122,7 @@
     q2_s[...] = jnp.zeros_like(q2_s)
     th_s[...] = jnp.zeros_like(th_s)
 
+    load.wait()
     step_cols = 2 * LANES
     for k in range(width // step_cols):
         cols = slice(k * step_cols, (k + 1) * step_cols)
@@ -185,6 +192,7 @@
         pg = (bi + bc) * st_s[p] * sig * (1.0 + pre * (1.0 - sig))
         pg = pg.astype(bf16).astype(f32)
         if ring:
+            pg_t[at, :] = jnp.transpose(pg).astype(bf16)
             pg_s[p, 0] = pg[:half]
             pg_s[p, 1] = pg[half:]
             for w in range(2):
@@ -201,7 +209,7 @@
         q1_s[...] += dot_exact(grad * y - x * bi, pick)
         q2_s[...] += dot_exact(x * bc, pick)
         through = jnp.exp(end) * jnp.sum(pr * ad, axis=0, keepdims=True)
-        th_s[...] += dot_exact(jnp.broadcast_to(through, (8, LANES)), pick)
+        th_s[...] += dot_exact(pick, jnp.broadcast_to(through, (8, LANES)), (((0,), (1,)), ((), ())))
 
     def forward(s):
         def one(k, carry):
@@ -247,12 +255,9 @@
             tokmat[...].reshape(n * rows, tokmat.shape[2]), jnp.concatenate(blocks, axis=0), ROWS)
 
     def input_part(o):
-        tcols = part.shape[2]
+        tcols = part.shape[1]
         to = lax.rem(h + o, nh)
-        pgb = jnp.concatenate(
-            [jnp.concatenate([pg_s[p, w].astype(bf16) for p in range(pairs)], axis=1)
-             for w in range(2)], axis=0)
-        part[o] = dot_f32(pgb, xw[pl.ds(pl.multiple_of(to * tcols, tcols), tcols), :], COLS)
+        part[o] = dot_f32(xw[pl.ds(pl.multiple_of(to * tcols, tcols), tcols), :], pg_t[...])
         if o:
             gcopy(o).start()
 
@@ -317,8 +322,8 @@
     lax.fori_loop(0, total_steps, chain, 0)
 
     strict_ones = (row_ids > col_ids).astype(f32)
-    dg_ref[...] = (dot_exact(lower_ones, q1_s[...], ROWS) + dot_exact(strict_ones, q2_s[...])
-                   + th_s[0:1, :])
+    dg_ref[...] = (dot_exact(q1_s[...], lower_ones, ROWS)
+                   + dot_exact(q2_s[...], strict_ones, (((0,), (1,)), ((), ()))) + th_s[:, 0:1])
 
     @pl.when(d < n - 1)
     def _():
@@ -344,7 +349,7 @@
         for o in range(1, nh):
             gcopy(o).wait()
             total = total + got[o]
-        tg_ref[...] = total.astype(bf16)
+        tg_ref[...] = jnp.transpose(total).astype(bf16)
 
         def drain(k, carry):
             for w in range(2):
@@ -364,7 +369,7 @@
     tokens, x_weight, b_input, _, log_decay, _, cotangent = args[:7]
     rows, width = cotangent.shape
     depth = tokens.shape[1]
-    heads, state = log_decay.shape[1], b_input.shape[1]
+    heads, state = log_decay.shape[0], b_input.shape[1]
     pairs = width // LANES
     vm = pl.BlockSpec(memory_space=pltpu.VMEM)
     wide = pltpu.VMEM((pairs, rows, LANES), f32)
@@ -373,18 +378,18 @@
     scratch = [
         pltpu.VMEM((pairs, rows, LANES), bf16), wide, wide, wide, pltpu.VMEM((heads, rows), f32),
         wide, wide, pltpu.VMEM((rows, rows), f32), states, states, states, states, states, states,
-        pltpu.VMEM((rows, heads), f32), pltpu.VMEM((rows, heads), f32), pltpu.VMEM((8, heads), f32),
-        dma((pairs,)), dma((pairs,)), dma((pairs,)), dma((pairs,))]
+        pltpu.VMEM((rows, heads), f32), pltpu.VMEM((rows, heads), f32), pltpu.VMEM((heads, 8), f32),
+        pltpu.VMEM(x_weight.shape, bf16), dma(()), dma((pairs,)), dma((pairs,)), dma((pairs,)), dma((pairs,))]
     y = jax.ShapeDtypeStruct((rows, width), bf16)
-    dg = jax.ShapeDtypeStruct((rows, heads), f32)
+    dg = jax.ShapeDtypeStruct((heads, rows), f32)
     if ring:
         cols, tcols = depth // n, depth // nh
         outs = [y, dg, jax.ShapeDtypeStruct((cols, width), f32), jax.ShapeDtypeStruct((rows, tcols), bf16)]
-        out_part = pltpu.VMEM((nh, rows, tcols), f32)
+        out_part = pltpu.VMEM((nh, tcols, rows), f32)
         scratch += [
-            pltpu.VMEM((pairs, 2, rows // 2, LANES), f32),
+            pltpu.VMEM((pairs, 2, rows // 2, LANES), f32), pltpu.VMEM((width, rows), bf16),
             pltpu.VMEM((n - 1, pairs, 2, rows // 2, LANES), f32),
-            pltpu.VMEM((nh,) + args[7].shape, f32), pltpu.VMEM((n, rows, cols), bf16), out_part, out_part,
+            pltpu.VMEM((n, rows // nh, cols), f32), pltpu.VMEM((nh, n, rows // nh, cols), f32), pltpu.VMEM((n, rows, cols), bf16), out_part, out_part,
             dma((n - 1, pairs, 2)), dma((n - 1, pairs, 2)), dma((n,)), dma((n,)),
             dma((nh,)), dma((nh,)), dma((nh,)), dma((nh,))]
     else:
@@ -392,7 +397,7 @@
     return pl.pallas_call(
         functools.partial(span_kernel, n, nh, ring),
         out_shape=outs,
-        in_specs=[vm] * len(args),
+        in_specs=[vm, pl.BlockSpec(memory_space=pl.ANY)] + [vm] * (len(args) - 2),
         out_specs=[vm] * len(outs),
         scratch_shapes=scratch,
         compiler_params=pltpu.CompilerParams(
@@ -403,23 +408,49 @@
     )(*args)
 
 
+def hand_kernel(count, *refs):
+    ins, outs, mids = refs[:count], refs[count:2 * count], refs[2 * count:3 * count]
+    sems = refs[3 * count]
+    first = [pltpu.make_async_copy(a, m, sems.at[0, i]) for i, (a, m) in enumerate(zip(ins, mids))]
+    second = [pltpu.make_async_copy(m, b, sems.at[1, i]) for i, (m, b) in enumerate(zip(mids, outs))]
+    for copy in first:
+        copy.start()
+    for one, two in zip(first, second):
+        one.wait()
+        two.start()
+    for copy in second:
+        copy.wait()
+
+
+def hand_over(*arrays):
+    anywhere = pl.BlockSpec(memory_space=pl.ANY)
+    count = len(arrays)
+    return pl.pallas_call(
+        functools.partial(hand_kernel, count),
+        out_shape=[jax.ShapeDtypeStruct(a.shape, a.dtype) for a in arrays],
+        in_specs=[anywhere] * count,
+        out_specs=[anywhere] * count,
+        scratch_shapes=[pltpu.VMEM(a.shape, a.dtype) for a in arrays]
+        + [pltpu.SemaphoreType.DMA((2, count))],
+        name="hand_over",
+    )(*arrays)
+
+
 def per_device(tokens, x_weight, b_input, c_input, log_decay, step_size, cotangent):
     n, nh = lax.axis_size("seq"), lax.axis_size("head")
     rows, depth = tokens.shape
     assert rows == SPAN and n % 2 == 0
     ring = 4 <= n <= 8
-    args = (tokens, x_weight, b_input, c_input, log_decay, step_size, cotangent)
-    if ring:
-        quarter = rows // nh
-        mine = lax.dynamic_slice_in_dim(tokens, lax.axis_index("head") * quarter, quarter, 0)
-        mine = jnp.transpose(mine.reshape(quarter, n, depth // n), (1, 0, 2)).astype(f32)
-        y, dg, wg, tg = span_call(n, nh, True, *args, mine)
-        return y, tg, wg, dg
+    args = (tokens, x_weight, b_input, c_input, log_decay.T, step_size.T, cotangent)
+    if ring:
+        y, dg, wg, tg = span_call(n, nh, True, *args)
+        y, wg, tg = hand_over(y, wg, tg)
+        return y, tg, wg, dg.T
     y, pg, dg = span_call(n, nh, False, *args)
     pgb = pg.astype(bf16)
     wg = lax.psum_scatter(dot_f32(tokens, pgb, ROWS), "seq", scatter_dimension=0, tiled=True)
     tg = lax.psum_scatter(dot_f32(pgb, x_weight, COLS), "head", scatter_dimension=1, tiled=True)
-    return y, tg.astype(bf16), wg, dg
+    return y, tg.astype(bf16), wg, dg.T
 
 
 def solution(mesh):

time: 187 us -> 175 us (0.936)
  local copies, waits for them, and re-layouts: 10.8 us -> 0.61 us
    unnamed x8 -> x3, local copies, waits for them, and re-layouts: 9.57 us -> 0.61 us
    pallas_call x1, Pallas kernels: 174 us -> 171 us  [span_call(): pl.pallas_call(functools.partial(span_kernel, n, nh, ring), out_shape=out...]
    pallas_call x0 -> x1, Pallas kernels: none -> 2.96 us  [hand_over(): pl.pallas_call(functools.partial(hand_kernel, count), out_shape=[jax.Shap...]
where the time goes in v3:
time: 175 us
  Pallas kernels  174 us (99%)
    pallas_call x1, Pallas kernels, span_call(): pl.pallas_call(functools.partial(span_kernel, n, nh, ring), out_shape=out...  171 us

profile of v3, /device:TPU:0, one launch (start us, length us, event | category | flops | bytes accessed | tf_op | source)
XLA Modules:
  0.0 175.0 jit_solution(9631939996259921844)
XLA Ops:
  0.6 170.8 %span.1 = (bf16[256,1280]{1,0:T(8,128)(2,1)}, f32[20,256]{1,0:T(8,128)}, f32[320,1280]{1,0:T(8,128)}, bf16[256,640]{1,0:T(8,128)(2,1)}) custom-call(bf16[256,2560]{1,0:T(8,128)(2,1)} %refs_0_.1, bf16[2560,1280]{1,0:T(8,128)(2,1)} %refs_1_.1, bf16[256,128]{1,0:T(8,128)(2,1)} %refs_2_.1, bf16[256,128]{1,0:T(8,128)(2,1)} %refs_3_.1, f32[20,256]{1,0:T(8,128)} %bitcast.4, ...), custom_call_target="tpu_custom_call" | custom-call | flops 5033164800 | bytes 12582912 | tf_op jit(solution)/shard_map/span/pallas_call | solution.py:397
  171.4 0.0 copy-start
  171.4 3.0 %hand_over.1 = (bf16[256,1280]{1,0:T(8,128)(2,1)}, f32[320,1280]{1,0:T(8,128)}, bf16[256,640]{1,0:T(8,128)(2,1)}) custom-call(bf16[256,1280]{1,0:T(8,128)(2,1)} %get-tuple-element.11.refs_0_, f32[320,1280]{1,0:T(8,128)} %get-tuple-element.12.refs_1_, bf16[256,640]{1,0:T(8,128)(2,1)} %get-tuple-element.13.refs_2_), custom_call_target="tpu_custom_call" | custom-call | tf_op jit(solution)/shard_map/hand_over/pallas_call | solution.py:428
  174.4 0.0 copy-done
  174.4 0.6 copy.12
Async XLA Ops:
  171.4 3.0 %copy-start = (f32[20,256]{1,0:T(8,128)S(1)}, f32[20,256]{1,0:T(8,128)}, u32[]{:S(2)}) copy-start(f32[20,256]{1,0:T(8,128)} %get-tuple-element.17) | copy-start | bytes 61444

commit v4 on v3

--- a/solution.py
+++ b/solution.py
@@ -179,12 +179,11 @@
         inner_s[p] = inner
         back_s[p] = back
 
-    def finish(p):
+    def finish_grad(p):
         ce = ce_s[p]
         end = ce[rows - 1:rows]
         at = pl.ds(pl.multiple_of(p * LANES, LANES), LANES)
-        pr, ad = prior[p], adj[p]
-        hi, lo = split_two(ad)
+        hi, lo = split_two(adj[p])
         bc = jnp.exp(end - ce) * (dot_f32(b_val, hi) + dot_f32(b_val, lo))
         bi = back_s[p]
         pre = pre_s[p]
@@ -199,25 +198,36 @@
                 hop(0, p, w, pg_s.at[p, w]).start()
         else:
             pg_ref[:, at] = pg
+        q2_s[...] += dot_exact(x_s[p].astype(f32) * bc, picker(p))
+
+    def picker(p):
+        return (lax.broadcasted_iota(jnp.int32, (LANES, heads), 0) // hdim + per * p
+                == lax.broadcasted_iota(jnp.int32, (LANES, heads), 1)).astype(f32)
+
+    def finish(p):
+        ce = ce_s[p]
+        end = ce[rows - 1:rows]
+        at = pl.ds(pl.multiple_of(p * LANES, LANES), LANES)
+        pr, ad = prior[p], adj[p]
+        bi = back_s[p]
         grad = cot[:, at].astype(f32)
         x = x_s[p].astype(f32)
         hi, lo = split_two(pr)
         y = inner_s[p] + jnp.exp(ce) * (dot_f32(c_val, hi) + dot_f32(c_val, lo))
         y_ref[:, at] = y.astype(bf16)
-        pick = (lax.broadcasted_iota(jnp.int32, (LANES, heads), 0) // hdim + per * p
-                == lax.broadcasted_iota(jnp.int32, (LANES, heads), 1)).astype(f32)
+        pick = picker(p)
         q1_s[...] += dot_exact(grad * y - x * bi, pick)
-        q2_s[...] += dot_exact(x * bc, pick)
         through = jnp.exp(end) * jnp.sum(pr * ad, axis=0, keepdims=True)
         th_s[...] += dot_exact(pick, jnp.broadcast_to(through, (8, LANES)), (((0,), (1,)), ((), ())))
 
     def forward(s):
-        def one(k, carry):
-            j = s - n - k
-
-            @pl.when(jnp.logical_and(j >= 0, j < n - 1))
-            def _():
-                for w in range(2):
+        def one(j, carry):
+            sources = (member(lax.rem(pos + n - 1 - j, n)), member(lax.rem(pos + 1 + j, n)))
+            for w in range(2):
+                k = s - (n - sources[w] + j)
+
+                @pl.when(jnp.logical_and(k >= 0, k < pairs))
+                def _():
                     hop(j, k, w, gat.at[j, k, w]).wait_recv()
 
                     @pl.when(j < n - 2)
@@ -226,7 +236,7 @@
 
             return carry
 
-        lax.fori_loop(0, pairs, one, 0)
+        lax.fori_loop(0, n - 1, one, 0)
 
     def arrange():
         for o in range(1, nh):
@@ -294,6 +304,10 @@
         def _():
             mix(s)
 
+        @pl.when(jnp.logical_and(kb >= 0, kb < pairs))
+        def _():
+            finish_grad(kb)
+
         ks = s - (n - 1)
 
         @pl.when(jnp.logical_and(ks >= 0, ks < pairs))
@@ -309,7 +323,7 @@
                     hcopy(o).start()
 
             for o in range(nh):
-                @pl.when(s == n - 1 + pairs + (o - 1) % nh)
+                @pl.when(s == n - 1 - d + pairs + (o - 1) % nh)
                 def _():
                     input_part(o)
 

time: 175 us -> 198 us (1.13)
  Pallas kernels: 174 us -> 196 us
    pallas_call x1, Pallas kernels: 171 us -> 193 us  [span_call(): pl.pallas_call(functools.partial(span_kernel, n, nh, ring), out_shape=out...]
where the time goes in v4:
time: 198 us; the launch traced here: 197 us
  Pallas kernels  196 us (99%)
    pallas_call x1, Pallas kernels, span_call(): pl.pallas_call(functools.partial(span_kernel, n, nh, ring), out_shape=out...  193 us

profile of v4, /device:TPU:0, one launch (start us, length us, event | category | flops | bytes accessed | tf_op | source)
XLA Modules:
  0.0 197.3 jit_solution(10472059248614219174)
XLA Ops:
  0.6 193.1 %span.1 = (bf16[256,1280]{1,0:T(8,128)(2,1)}, f32[20,256]{1,0:T(8,128)}, f32[320,1280]{1,0:T(8,128)}, bf16[256,640]{1,0:T(8,128)(2,1)}) custom-call(bf16[256,2560]{1,0:T(8,128)(2,1)} %refs_0_.1, bf16[2560,1280]{1,0:T(8,128)(2,1)} %refs_1_.1, bf16[256,128]{1,0:T(8,128)(2,1)} %refs_2_.1, bf16[256,128]{1,0:T(8,128)(2,1)} %refs_3_.1, f32[20,256]{1,0:T(8,128)} %bitcast.4, ...), custom_call_target="tpu_custom_call" | custom-call | flops 5033164800 | bytes 12582912 | tf_op jit(solution)/shard_map/span/pallas_call | solution.py:411
  193.7 0.0 copy-start
  193.7 3.0 %hand_over.1 = (bf16[256,1280]{1,0:T(8,128)(2,1)}, f32[320,1280]{1,0:T(8,128)}, bf16[256,640]{1,0:T(8,128)(2,1)}) custom-call(bf16[256,1280]{1,0:T(8,128)(2,1)} %get-tuple-element.11.refs_0_, f32[320,1280]{1,0:T(8,128)} %get-tuple-element.12.refs_1_, bf16[256,640]{1,0:T(8,128)(2,1)} %get-tuple-element.13.refs_2_), custom_call_target="tpu_custom_call" | custom-call | tf_op jit(solution)/shard_map/hand_over/pallas_call | solution.py:442
  196.7 0.0 copy-done
  196.7 0.6 copy.12
Async XLA Ops:
  193.7 3.0 %copy-start = (f32[20,256]{1,0:T(8,128)S(1)}, f32[20,256]{1,0:T(8,128)}, u32[]{:S(2)}) copy-start(f32[20,256]{1,0:T(8,128)} %get-tuple-element.17) | copy-start | bytes 61444
